TPU v7x, 256 devices: a whole 4x4x8 slice. The times are simulated.
256 devices in a mesh: seq: 16 (over z, core), mp: 8 (over y, x_hi), dp: 2 (over x_lo).
Axes of the slice: x: 4 (x_hi: 2, x_lo: 2; x = x_hi * 2 + x_lo), y: 4, z: 8, core: 2. Of those that a mesh axis runs over, the one named last changes fastest.
Arguments:
- latents: bfloat16 [2, 3072, 1792], P('dp', 'seq', 'mp'), may hold values from -6 to 6
- grad_out: bfloat16 [2, 3072, 1792], P('dp', 'seq', 'mp'), may hold values from -6 to 6
- sync_mod: bfloat16 [2, 2400, 3584], P('dp', 'seq'), may hold values from -3 to 3
- w_qkv: bfloat16 [1792, 3, 1024], P(None, None, 'mp'), may hold values from -0.125 to 0.125
- w_out: bfloat16 [1024, 1792], P('mp'), may hold values from -0.1875 to 0.1875
- q_gain: float32 [8, 128], P('mp'), may hold values from 0.5 to 2.5
- k_gain: float32 [8, 128], P('mp'), may hold values from 0.5 to 2.5
- frame_of: int32 [2, 3072], P('dp', 'seq'), may hold values from 0 to 2399, as said below
- group_id: int32 [2, 3072], P('dp'), may hold values from 0 to 63, never falling along the last dimension, each value on 1 to 96 neighbouring positions
- clip_len: int32 [2], P('dp'), may hold values from 1536 to 3072
Outputs:
- mixed: bfloat16 [2, 3072, 1792], P('dp', 'seq', 'mp')
- grad_latents: bfloat16 [2, 3072, 1792], P('dp', 'seq', 'mp')
- grad_wqkv: float32 [1792, 3, 1024], P(('seq', 'dp'), None, 'mp')
- grad_wout: float32 [1024, 1792], P('mp', ('seq', 'dp'))
Inputs may be any that keep to these rules, and one draw needn't show every extreme that they name: frame_of[c, l] = floor((96 l + s) / 125) with a phase s of 0 to 124 drawn for each clip, so the latents on seq index j read frames held by seq indices j - 1 and j only.
All inputs are finite; a program needn't handle non-finite values.
Results may differ from a plain program's by a relative error of at most 0.012.
The roundings to bfloat16 on the way count: a program that leaves them out, or rounds other values in their place, can miss the bound.
Values may be sent and summed in bfloat16 or wider, within the bound.
A program may use at most 64 MiB of HBM per device.

v0:
```python
import jax
import jax.numpy as jnp
from jax import lax
from jax.sharding import PartitionSpec as P

EPSILON = 1e-06
NEG_FILL = -1e30


def from_behind(value, axis, steps):
    count = lax.axis_size(axis)
    leading, last = (max(0, -steps), min(count, count - steps))
    return lax.ppermute(value, axis, [(source, source + steps) for source in range(leading, last)])


def inv_rms(values):
    return lax.rsqrt(jnp.mean(values * values, axis=-1, keepdims=True) + EPSILON)


def norm_back(raw, inv_norm, gains, upstream):
    inner_dot = jnp.mean(upstream * gains * raw, axis=-1, keepdims=True)
    return inv_norm * (gains * upstream - raw * inv_norm * inv_norm * inner_dot)


def group_mask(group_ids, clip_length, query_first, query_span, key_span):
    query_group = lax.dynamic_slice_in_dim(group_ids, query_first, query_span, 1)
    key_place = lax.iota(jnp.int32, key_span)
    allowed = (group_ids[:, None, :] <= query_group[:, :, None]) & (
        key_place[None, None, :] < clip_length[:, None, None]
    )
    return allowed[:, None, :, :]


def head_logits(queries, keys, factor):
    return jnp.einsum("cqhd,ckhd->chqk", queries, keys, preferred_element_type=jnp.float32) * factor


def on_device(
    latents, grad_out, sync_mod, w_qkv, w_out, q_gain, k_gain, frame_of, group_id, clip_len
):
    clip_count, row_count, width_part = latents.shape
    frame_count = sync_mod.shape[1]
    model_width = sync_mod.shape[2] // 2
    heads_here, head_dim = q_gain.shape
    inner_width = heads_here * head_dim
    factor = head_dim ** (-0.5)
    seq_place = lax.axis_index("seq")
    model_place = lax.axis_index("mp")
    query_first = seq_place * row_count
    inputs_full, upstream_full = (
        lax.all_gather(latents, "mp", axis=2, tiled=True),
        lax.all_gather(grad_out, "mp", axis=2, tiled=True),
    )
    earlier = from_behind(sync_mod, "seq", 1)
    window = jnp.concatenate([earlier, sync_mod], axis=1)
    local_frame = frame_of - (seq_place * frame_count - frame_count)
    selector = (
        local_frame[:, :, None] == lax.iota(jnp.int32, 2 * frame_count)[None, None, :]
    ).astype(jnp.bfloat16)
    modulation = jnp.einsum("clf,cfe->cle", selector, window, preferred_element_type=jnp.float32)
    mod_scale = modulation[:, :, :model_width]
    mod_gate = modulation[:, :, model_width:]
    inputs_f = inputs_full.astype(jnp.float32)
    inv_norm = inv_rms(inputs_f)
    normed = inputs_f * inv_norm
    hidden = (normed * (1.0 + mod_scale)).astype(jnp.bfloat16)
    flat_hidden = hidden.reshape(clip_count * row_count, model_width)
    flat_weight = w_qkv.reshape(model_width, 3 * inner_width)
    projected = jnp.dot(flat_hidden, flat_weight, preferred_element_type=jnp.float32)
    projected = projected.reshape(clip_count, row_count, 3, heads_here, head_dim)
    query_raw = projected[:, :, 0]
    key_raw = projected[:, :, 1]
    query_inv = inv_rms(query_raw)
    key_inv = inv_rms(key_raw)
    query_norm = (query_raw * query_inv * q_gain).astype(jnp.bfloat16)
    key_norm = (key_raw * key_inv * k_gain).astype(jnp.bfloat16)
    values = projected[:, :, 2].astype(jnp.bfloat16)
    row_max = jnp.full((clip_count, heads_here, row_count), NEG_FILL, jnp.float32)
    key_piece = lax.all_gather(key_norm, "seq", axis=1, tiled=True)
    value_piece = lax.all_gather(values, "seq", axis=1, tiled=True)
    span_len = key_piece.shape[1]
    allowed = group_mask(group_id, clip_len, query_first, row_count, span_len)
    logits = jnp.where(allowed, head_logits(query_norm, key_piece, factor), NEG_FILL)
    new_max = jnp.maximum(row_max, jnp.max(logits, axis=-1))
    unnorm = jnp.where(allowed, jnp.exp(logits - new_max[..., None]), 0.0)
    row_sum = jnp.sum(unnorm, axis=-1)
    row_acc = jnp.einsum(
        "chqk,ckhd->chqd",
        unnorm.astype(jnp.bfloat16),
        value_piece,
        preferred_element_type=jnp.float32,
    )
    row_max, row_sum, row_acc = (new_max, row_sum, row_acc)
    key_all, value_all = (
        lax.all_gather(key_norm, "seq", axis=1, tiled=True),
        lax.all_gather(values, "seq", axis=1, tiled=True),
    )
    heads_out = jnp.transpose(row_acc / row_sum[..., None], (0, 2, 1, 3)).astype(jnp.bfloat16)
    out_rows = heads_out.reshape(clip_count * row_count, inner_width)
    attn_part = jnp.dot(out_rows, w_out, preferred_element_type=jnp.float32).reshape(
        clip_count, row_count, model_width
    )
    attn_mine = lax.psum_scatter(attn_part, "mp", scatter_dimension=2, tiled=True)
    gate_mine = lax.dynamic_slice_in_dim(mod_gate, model_place * width_part, width_part, 2)
    mixed = (latents.astype(jnp.float32) + gate_mine * attn_mine).astype(jnp.bfloat16)
    grad_attn = (upstream_full.astype(jnp.float32) * mod_gate).astype(jnp.bfloat16)
    flat_grad = grad_attn.reshape(clip_count * row_count, model_width)
    grad_wout = jnp.einsum("ti,td->id", out_rows, flat_grad, preferred_element_type=jnp.float32)
    grad_heads = jnp.einsum(
        "td,id->ti", flat_grad, w_out, preferred_element_type=jnp.float32
    ).astype(jnp.bfloat16)
    grad_heads = grad_heads.reshape(clip_count, row_count, heads_here, head_dim)
    out_dot = jnp.transpose(
        jnp.sum(grad_heads.astype(jnp.float32) * heads_out.astype(jnp.float32), axis=-1), (0, 2, 1)
    )
    allowed_all = group_mask(group_id, clip_len, query_first, row_count, key_all.shape[1])
    logits_all = head_logits(query_norm, key_all, factor)
    probs = jnp.where(
        allowed_all, jnp.exp(logits_all - row_max[..., None]) / row_sum[..., None], 0.0
    )
    grad_probs = jnp.einsum(
        "cqhd,ckhd->chqk", grad_heads, value_all, preferred_element_type=jnp.float32
    )
    grad_logits = (probs * (grad_probs - out_dot[..., None])).astype(jnp.bfloat16)
    grad_qnorm = (
        jnp.einsum("chqk,ckhd->cqhd", grad_logits, key_all, preferred_element_type=jnp.float32)
        * factor
    )
    grad_key_all = (
        jnp.einsum("chqk,cqhd->ckhd", grad_logits, query_norm, preferred_element_type=jnp.float32)
        * factor
    )
    grad_value_all = jnp.einsum(
        "chqk,cqhd->ckhd",
        probs.astype(jnp.bfloat16),
        grad_heads,
        preferred_element_type=jnp.float32,
    )
    key_terms = jnp.stack([grad_key_all, grad_value_all], axis=2)
    key_share = lax.psum_scatter(key_terms, "seq", scatter_dimension=1, tiled=True)
    grad_knorm = key_share[:, :, 0]
    grad_values = key_share[:, :, 1]
    grad_query = norm_back(query_raw, query_inv, q_gain, grad_qnorm)
    grad_key = norm_back(key_raw, key_inv, k_gain, grad_knorm)
    grad_proj = jnp.stack([grad_query, grad_key, grad_values], axis=2).astype(jnp.bfloat16)
    grad_proj = grad_proj.reshape(clip_count * row_count, 3 * inner_width)
    grad_wqkv = jnp.einsum(
        "te,tf->ef", flat_hidden, grad_proj, preferred_element_type=jnp.float32
    ).reshape(model_width, 3, inner_width)
    grad_wqkv, grad_wout = (
        lax.psum_scatter(grad_wqkv, ("seq", "dp"), scatter_dimension=0, tiled=True),
        lax.psum_scatter(grad_wout, ("seq", "dp"), scatter_dimension=1, tiled=True),
    )
    grad_hidden = jnp.einsum(
        "tf,ef->te", grad_proj, flat_weight, preferred_element_type=jnp.float32
    )
    grad_hidden = grad_hidden.reshape(clip_count, row_count, model_width)
    grad_full = lax.psum(grad_hidden, "mp")
    grad_normed = grad_full * (1.0 + mod_scale)
    grad_whole = inv_norm * (
        grad_normed - normed * jnp.mean(grad_normed * normed, axis=-1, keepdims=True)
    )
    grad_inputs = lax.dynamic_slice_in_dim(grad_whole, model_place * width_part, width_part, 2)
    grad_latents = (grad_out.astype(jnp.float32) + grad_inputs).astype(jnp.bfloat16)
    return (mixed, grad_latents, grad_wqkv, grad_wout)


def solution(mesh):
    in_specs = (
        P("dp", "seq", "mp"),
        P("dp", "seq", "mp"),
        P("dp", "seq", None),
        P(None, None, "mp"),
        P("mp", None),
        P("mp", None),
        P("mp", None),
        P("dp", "seq"),
        P("dp", None),
        P("dp"),
    )
    out_specs = (
        P("dp", "seq", "mp"),
        P("dp", "seq", "mp"),
        P(("seq", "dp"), None, "mp"),
        P("mp", ("seq", "dp")),
    )
    return jax.shard_map(
        on_device, mesh=mesh, in_specs=in_specs, out_specs=out_specs, check_vma=False
    )
```

profile of v0, /device:TPU:1, one launch (start us, length us, event | category | flops | bytes accessed | tf_op | source)
XLA Modules:
  0.0 658.3 jit_solution(18341032263958154900)
XLA Ops:
  7.2 5.1 collective-permute-start
  12.9 1.1 copy.23
  14.0 1.1 copy.27
  15.1 2.6 copy.25
  17.7 41.4 %all_gather.17 = bf16[1,192,1792]{1,0,2:T(2,128)(2,1)S(1)} all-gather(bf16[1,192,224]{1,0,2:T(2,128)(2,1)S(1)} %copy.27), channel_id=1, replica_groups=mesh['seq'=16,'mp'=8,'dp'=2] {'mp'}, dimensions={2}, use_global_device_ids=true | all-gather | bytes 774144 | tf_op jit(solution)/shard_map/all_gather | solution.py:52
  59.0 3.8 copy.28
  62.9 38.2 %all_gather.14 = bf16[1,192,1792]{1,0,2:T(2,128)(2,1)S(1)} all-gather(bf16[1,192,224]{1,0,2:T(2,128)(2,1)S(1)} %copy.23), channel_id=1, replica_groups=mesh['seq'=16,'mp'=8,'dp'=2] {'mp'}, dimensions={2}, use_global_device_ids=true | all-gather | bytes 774144 | tf_op jit(solution)/shard_map/all_gather | solution.py:51
  101.1 4.0 copy.24
  105.9 2.6 convolution_bitcast_fusion
  108.5 1.4 convert_multiply_fusion
  110.9 28.8 %all-gather = bf16[1,3072,1,1,128]{4,1,2,3,0:T(8,128)(2,1)S(1)} all-gather(bf16[1,192,1,1,128]{4,1,2,3,0:T(8,128)(2,1)S(1)} %slice.67), channel_id=2, replica_groups=mesh['seq'=16,'mp'=8,'dp'=2] {'seq'}, dimensions={1}, use_global_device_ids=true | all-gather | bytes 835584 | tf_op jit(solution)/shard_map/all_gather | solution.py:80
  139.8 17.0 %all_gather.15 = bf16[1,3072,1,128]{3,1,2,0:T(8,128)(2,1)S(1)} all-gather(bf16[1,192,1,128]{3,1,2,0:T(8,128)(2,1)S(1)} %fusion.47), channel_id=1, replica_groups=mesh['seq'=16,'mp'=8,'dp'=2] {'seq'}, dimensions={1}, use_global_device_ids=true | all-gather | bytes 835584 | tf_op jit(solution)/shard_map/all_gather | solution.py:79
  159.0 1.2 convolution_bitcast_fusion.1
  160.2 1.0 multiply_reduce_fusion.1
  161.3 1.1 fusion.1
  164.2 1.9 pad_maximum_fusion
  166.2 1.4 convolution_bitcast_fusion.3
  167.6 5.1 copy.35
  172.6 2.9 copy.52
  175.8 2.0 fusion.54
  178.7 42.9 %reduce-scatter.10.cloned.1.call-done = f32[1,192,2,1,128]{4,1,2,3,0:T(8,128)} async-done(((f32[1,3072,2,1,128]{4,1,2,3,0:T(8,128)}), f32[1,192,2,1,128]{4,1,2,3,0:T(8,128)}) %reduce-scatter.10.cloned.1.call-update) | async-done | bytes 196624 | tf_op jit(solution)/shard_map/reduce_scatter | solution.py:140
  222.6 1.1 subtract_multiply_fusion
  223.8 3.0 convolution_bitcast_fusion.2
  226.9 2.6 fusion.67
  229.5 3.3 fusion.36
  232.9 72.6 %reduce-scatter.14.cloned.1.call-done = f32[224,192]{1,0:T(8,128)} async-done(((f32[1792,192]{1,0:T(8,128)}), f32[224,192]{1,0:T(8,128)}) %reduce-scatter.14.cloned.1.call-update) | async-done | bytes 172048
  305.5 1.1 reshape_bitcast_fusion
  307.4 94.9 %all-reduce.3.cloned.1.call-done = f32[1,192,1792]{2,1,0:T(8,128)} async-done(((f32[1,192,1792]{2,1,0:T(8,128)}), f32[1,192,1792]{2,1,0:T(8,128)}) %all-reduce.3.cloned.1.call-update) | async-done | bytes 1376272 | tf_op jit(solution)/shard_map/psum | solution.py:158
  402.3 2.0 multiply_reduce_fusion
  404.3 1.8 fusion.34
  406.9 119.1 %reduce-scatter.16.cloned.1.call-done = f32[128,56]{0,1:T(8,128)} async-done(((f32[128,1792]{0,1:T(8,128)}), f32[128,56]{0,1:T(8,128)}) %reduce-scatter.16.cloned.1.call-update) | async-done | bytes 28688
  526.1 125.7 %reduce-scatter.12.cloned.1.call-done = f32[56,3,128]{2,0,1:T(8,128)} async-done(((f32[1792,3,128]{2,0,1:T(8,128)}), f32[56,3,128]{2,0,1:T(8,128)}) %reduce-scatter.12.cloned.1.call-update) | async-done | bytes 86032 | tf_op jit(solution)/shard_map/reduce_scatter | solution.py:151
  (84 shorter events, 10.0 us)
Async XLA Ops:
  7.2 150.5 %copy-start = (bf16[128,1792]{1,0:T(8,128)(2,1)S(1)}, bf16[128,1792]{1,0:T(8,128)(2,1)}, u32[]{:S(2)}) copy-start(bf16[128,1792]{1,0:T(8,128)(2,1)} %param.14) | copy-start | bytes 1376260
  7.2 214.4 %reduce-scatter.10.cloned.1.call-start = ((), (), s32[]{:S(2)}) async-start(), calls=%async_computation.4 | async-start | bytes 3342336 | tf_op jit(solution)/shard_map/reduce_scatter | solution.py:140
  7.2 98.2 %collective-permute-start = (bf16[1,150,3584]{2,1,0:T(8,128)(2,1)}, bf16[1,150,3584]{2,1,0:T(8,128)(2,1)}, u32[]{:S(2)}, u32[]{:S(2)}) collective-permute-start(bf16[1,150,3584]{2,1,0:T(8,128)(2,1)} %param.12), channel_id=1, source_target_pairs={{0,16},{16,32},{32,48},{48,64},{64,80},{80,96},{96,112},{112,128},... | collective-permute-start | bytes 3225608 | tf_op jit(solution)/shard_map/ppermute | solution.py:13
  62.9 42.2 %copy-start.15 = (s32[1,3072]{1,0:T(1,128)S(1)}, s32[1,3072]{1,0:T(1,128)}, u32[]{:S(2)}) copy-start(s32[1,3072]{1,0:T(1,128)} %param.18) | copy-start | bytes 36868
  62.9 42.5 %copy-start.20 = (s32[1,192]{1,0:T(1,128)S(1)}, s32[1,192]{1,0:T(1,128)}, u32[]{:S(2)}) copy-start(s32[1,192]{1,0:T(1,128)} %param.17) | copy-start | bytes 2308
  105.0 0.9 copy-start.2
  105.4 3.1 copy-start.13
  105.9 2.6 copy-start.3
  108.5 1.6 copy-start.1
  109.9 46.9 %copy-start.5 = (bf16[192,1792,1]{1,0,2:T(8,128)(2,1)}, bf16[192,1792,1]{1,0,2:T(8,128)(2,1)S(1)}, u32[]{:S(2)}) copy-start(bf16[192,1792,1]{1,0,2:T(8,128)(2,1)S(1)} %get-tuple-element.8) | copy-start | bytes 2064388
  109.9 29.9 %copy-start.19 = (f32[1,128]{1,0:T(1,128)S(1)}, f32[1,128]{1,0:T(1,128)}, u32[]{:S(2)}) copy-start(f32[1,128]{1,0:T(1,128)} %param.16) | copy-start | bytes 1540
  110.0 46.8 %copy-start.21 = (f32[1,128]{1,0:T(1,128)S(1)}, f32[1,128]{1,0:T(1,128)}, u32[]{:S(2)}) copy-start(f32[1,128]{1,0:T(1,128)} %param.15) | copy-start | bytes 1540
  110.8 46.9 %copy-start.17 = (f32[192]{0:T(256)}, f32[192]{0:T(256)S(1)}, u32[]{:S(2)}) copy-start(f32[192]{0:T(256)S(1)} %add_rsqrt_fusion) | copy-start | bytes 2308
  110.9 51.4 %copy-start.18 = (f32[192]{0:T(256)}, f32[192]{0:T(256)S(1)}, u32[]{:S(2)}) copy-start(f32[192]{0:T(256)S(1)} %add_rsqrt_fusion.1) | copy-start | bytes 2308
  139.8 17.9 %copy-start.4 = (bf16[1,192,1792]{2,1,0:T(8,128)(2,1)S(1)}, bf16[1,192,1792]{2,1,0:T(8,128)(2,1)}, u32[]{:S(2)}) copy-start(bf16[1,192,1792]{2,1,0:T(8,128)(2,1)} %copy.28) | copy-start | bytes 2064388
  156.8 1.2 copy-start.7
  159.0 1.2 copy-start.16
  161.3 4.9 copy-start.11
  162.4 1.0 copy-start.6
  166.1 139.4 %reduce-scatter.14.cloned.1.call-start = ((), (), s32[]{:S(2)}) async-start(), calls=%async_computation.7 | async-start | bytes 2064384
  172.6 3.1 copy-start.22
  175.5 226.8 %all-reduce.3.cloned.1.call-start = ((), (), s32[]{:S(2)}) async-start(), calls=%async_computation.5 | async-start | bytes 2752512 | tf_op jit(solution)/shard_map/psum | solution.py:158
  223.8 3.1 copy-start.12
  226.8 299.2 %reduce-scatter.16.cloned.1.call-start = ((), (), s32[]{:S(2)}) async-start(), calls=%async_computation.8 | async-start | bytes 946176
  229.5 422.3 %reduce-scatter.12.cloned.1.call-start = ((), (), s32[]{:S(2)}) async-start(), calls=%async_computation.6 | async-start | bytes 2838528 | tf_op jit(solution)/shard_map/reduce_scatter | solution.py:151
  232.9 169.4 %copy-start.14 = (f32[192]{0:T(256)S(1)}, f32[192]{0:T(256)}, u32[]{:S(2)}) copy-start(f32[192]{0:T(256)} %copy-done.13) | copy-start | bytes 2308
  307.4 96.9 %copy-start.9 = (bf16[1,192,224]{2,1,0:T(8,128)(2,1)S(1)}, bf16[1,192,224]{2,1,0:T(8,128)(2,1)}, u32[]{:S(2)}) copy-start(bf16[1,192,224]{2,1,0:T(8,128)(2,1)} %param.11) | copy-start | bytes 258052
  307.4 98.8 %copy-start.8 = (f32[1,192,224]{2,1,0:T(8,128)S(1)}, f32[1,192,224]{2,1,0:T(8,128)}, u32[]{:S(2)}) copy-start(f32[1,192,224]{2,1,0:T(8,128)} %copy.36) | copy-start | bytes 516100
  402.3 3.8 copy-start.10
Sparse Core Ops, SparseCore 0:
  166.2 55.2 reduce-scatter.9
  225.6 79.8 reduce-scatter.13
  308.1 94.1 all-reduce.2
  405.2 120.7 reduce-scatter.15
  529.0 122.6 reduce-scatter.11
where the time goes:
time: 659 us; the launch traced here: 658 us
  waiting for transfers between devices  455 us (69%)
  blocking collectives  125 us (19%)
  local copies, waits for them, and re-layouts  24.3 us (4%)
  matrix products  20.9 us (3%)
  between operations  14.8 us (2%)
  other arithmetic  12.2 us (2%)
    unnamed x7, waiting for transfers between devices  192 us
    reduce_scatter x1, waiting for transfers between devices, on_device(): lax.psum_scatter(grad_wqkv, ('seq', 'dp'), scatter_dimension=0, tiled=True)  126 us
    psum x1, waiting for transfers between devices, on_device(): grad_full = lax.psum(grad_hidden, 'mp')  94.9 us
    reduce_scatter x1, waiting for transfers between devices, on_device(): lax.psum_scatter(key_terms, 'seq', scatter_dimension=1, tiled=True)  42.9 us
    all_gather x1, blocking collectives, on_device(): lax.all_gather(grad_out, 'mp', axis=2, tiled=True)  41.4 us
    all_gather x1, blocking collectives, on_device(): lax.all_gather(latents, 'mp', axis=2, tiled=True)  38.2 us
    all_gather x1, blocking collectives, on_device(): value_piece = lax.all_gather(values, 'seq', axis=1, tiled=True)  28.8 us
    all_gather x1, blocking collectives, on_device(): key_piece = lax.all_gather(key_norm, 'seq', axis=1, tiled=True)  17 us
  transfers between devices with their start and end apart: 6, of which 5 were waited for; matrix products, arithmetic and copies ran while one was open for 6% of the time, Pallas kernels for 0%

commit v1 on v0

--- a/solution.py
+++ b/solution.py
@@ -5,6 +5,12 @@
 
 EPSILON = 1e-06
 NEG_FILL = -1e30
+
+
+def gather_and_add(array, axis):
+    parts = lax.all_gather(array, axis, axis=0, tiled=False)
+    total = parts.sum(axis=0)
+    return total
 
 
 def from_behind(value, axis, steps):
@@ -155,7 +161,7 @@
         "tf,ef->te", grad_proj, flat_weight, preferred_element_type=jnp.float32
     )
     grad_hidden = grad_hidden.reshape(clip_count, row_count, model_width)
-    grad_full = lax.psum(grad_hidden, "mp")
+    grad_full = gather_and_add(grad_hidden, "mp")
     grad_normed = grad_full * (1.0 + mod_scale)
     grad_whole = inv_norm * (
         grad_normed - normed * jnp.mean(grad_normed * normed, axis=-1, keepdims=True)

time: 659 us -> 694 us (1.053)
  waiting for transfers between devices: 455 us -> 485 us
    all_gather x0 -> x1, waiting for transfers between devices: none -> 135 us  [gather_and_add(): parts = lax.all_gather(array, axis, axis=0, tiled=False)]
    psum x1 -> x0, waiting for transfers between devices: 94.9 us -> none  [on_device(): grad_full = lax.psum(grad_hidden, 'mp')]
    all_gather x1, blocking collectives: 17 us -> 28.8 us  [on_device(): key_piece = lax.all_gather(key_norm, 'seq', axis=1, tiled=True)]
    all_gather x1, blocking collectives: 28.8 us -> 17 us  [on_device(): value_piece = lax.all_gather(values, 'seq', axis=1, tiled=True)]
    unnamed x7, waiting for transfers between devices: 192 us -> 181 us
    unnamed x53 -> x55, local copies, waits for them, and re-layouts: 16.3 us -> 15.2 us
  transfers between devices with their start and end apart: 6 -> 6, of which waited for: 5 -> 5; matrix products, arithmetic and copies ran while one was open for 6% -> 7% of each run, Pallas kernels for 0% -> 0%
where the time goes in v1:
time: 694 us; the launch traced here: 693 us
  waiting for transfers between devices  485 us (70%)
  blocking collectives  125 us (18%)
  local copies, waits for them, and re-layouts  23.2 us (3%)
  matrix products  20.9 us (3%)
  other arithmetic  18.5 us (3%)
  between operations  14.9 us (2%)
    unnamed x7, waiting for transfers between devices  181 us
    all_gather x1, waiting for transfers between devices, gather_and_add(): parts = lax.all_gather(array, axis, axis=0, tiled=False)  135 us
    reduce_scatter x1, waiting for transfers between devices, on_device(): lax.psum_scatter(grad_wqkv, ('seq', 'dp'), scatter_dimension=0, tiled=True)  126 us
    reduce_scatter x1, waiting for transfers between devices, on_device(): lax.psum_scatter(key_terms, 'seq', scatter_dimension=1, tiled=True)  42.9 us
    all_gather x1, blocking collectives, on_device(): lax.all_gather(latents, 'mp', axis=2, tiled=True)  41.4 us
    all_gather x1, blocking collectives, on_device(): lax.all_gather(grad_out, 'mp', axis=2, tiled=True)  38 us
    all_gather x1, blocking collectives, on_device(): key_piece = lax.all_gather(key_norm, 'seq', axis=1, tiled=True)  28.8 us
    all_gather x1, blocking collectives, on_device(): value_piece = lax.all_gather(values, 'seq', axis=1, tiled=True)  17 us
  transfers between devices with their start and end apart: 6, of which 5 were waited for; matrix products, arithmetic and copies ran while one was open for 7% of the time, Pallas kernels for 0%

profile of v1, /device:TPU:1, one launch (start us, length us, event | category | flops | bytes accessed | tf_op | source)
XLA Modules:
  0.0 693.1 jit_solution(4557736066117866007)
XLA Ops:
  7.2 5.1 collective-permute-start
  12.3 1.1 copy.23
  13.4 41.4 %all_gather.17 = bf16[1,192,1792]{1,0,2:T(2,128)(2,1)S(1)} all-gather(bf16[1,192,224]{1,0,2:T(2,128)(2,1)S(1)} %copy.23), channel_id=1, replica_groups=mesh['seq'=16,'mp'=8,'dp'=2] {'mp'}, dimensions={2}, use_global_device_ids=true | all-gather | bytes 774144 | tf_op jit(solution)/shard_map/all_gather | solution.py:57
  54.8 4.0 copy.24
  58.7 2.8 copy.25
  62.4 38.0 %all_gather.20 = bf16[1,192,1792]{1,0,2:T(2,128)(2,1)S(1)} all-gather(bf16[1,192,224]{1,0,2:T(2,128)(2,1)S(1)} %copy.27), channel_id=1, replica_groups=mesh['seq'=16,'mp'=8,'dp'=2] {'mp'}, dimensions={2}, use_global_device_ids=true | all-gather | bytes 774144 | tf_op jit(solution)/shard_map/all_gather | solution.py:58
  100.4 3.8 copy.28
  104.6 2.6 convolution_bitcast_fusion
  107.2 1.4 convert_multiply_fusion
  109.6 28.8 %all_gather.18 = bf16[1,3072,1,128]{3,1,2,0:T(8,128)(2,1)S(1)} all-gather(bf16[1,192,1,128]{3,1,2,0:T(8,128)(2,1)S(1)} %fusion.47), channel_id=1, replica_groups=mesh['seq'=16,'mp'=8,'dp'=2] {'seq'}, dimensions={1}, use_global_device_ids=true | all-gather | bytes 835584 | tf_op jit(solution)/shard_map/all_gather | solution.py:85
  139.5 17.0 %all-gather = bf16[1,3072,1,1,128]{4,1,2,3,0:T(8,128)(2,1)S(1)} all-gather(bf16[1,192,1,1,128]{4,1,2,3,0:T(8,128)(2,1)S(1)} %slice.67), channel_id=2, replica_groups=mesh['seq'=16,'mp'=8,'dp'=2] {'seq'}, dimensions={1}, use_global_device_ids=true | all-gather | bytes 835584 | tf_op jit(solution)/shard_map/all_gather | solution.py:86
  157.8 1.2 convolution_bitcast_fusion.1
  160.0 1.1 fusion.1
  161.2 1.1 copy-done.6
  163.1 2.0 pad_maximum_fusion
  165.2 1.4 convolution_bitcast_fusion.2
  166.7 5.1 copy.35
  171.7 2.8 copy.52
  174.8 2.0 fusion.54
  177.7 42.9 %reduce-scatter.10.cloned.1.call-done = f32[1,192,2,1,128]{4,1,2,3,0:T(8,128)} async-done(((f32[1,3072,2,1,128]{4,1,2,3,0:T(8,128)}), f32[1,192,2,1,128]{4,1,2,3,0:T(8,128)}) %reduce-scatter.10.cloned.1.call-update) | async-done | bytes 196624 | tf_op jit(solution)/shard_map/reduce_scatter | solution.py:146
  221.6 1.1 subtract_multiply_fusion
  222.9 3.0 fusion.34
  225.9 2.5 fusion.67
  228.5 3.4 fusion.36
  232.0 72.6 %reduce-scatter.14.cloned.1.call-done = f32[224,192]{1,0:T(8,128)} async-done(((f32[1792,192]{1,0:T(8,128)}), f32[224,192]{1,0:T(8,128)}) %reduce-scatter.14.cloned.1.call-update) | async-done | bytes 172048
  304.6 1.1 reshape_bitcast_fusion
  306.5 135.4 %all-gather.4.cloned.1.call-done = f32[1536,1792]{1,0:T(8,128)} async-done(((f32[192,1792]{1,0:T(8,128)}), f32[1536,1792]{1,0:T(8,128)}) %all-gather.4.cloned.1.call-update) | async-done | bytes 11010064 | tf_op jit(solution)/shard_map/all_gather | solution.py:11
  441.9 6.0 reduce.13
  447.9 2.0 multiply_reduce_fusion
  449.9 1.8 fusion.33
  452.5 108.4 %reduce-scatter.16.cloned.1.call-done = f32[128,56]{0,1:T(8,128)} async-done(((f32[128,1792]{0,1:T(8,128)}), f32[128,56]{0,1:T(8,128)}) %reduce-scatter.16.cloned.1.call-update) | async-done | bytes 28688
  560.9 125.7 %reduce-scatter.12.cloned.1.call-done = f32[56,3,128]{2,0,1:T(8,128)} async-done(((f32[1792,3,128]{2,0,1:T(8,128)}), f32[56,3,128]{2,0,1:T(8,128)}) %reduce-scatter.12.cloned.1.call-update) | async-done | bytes 86032 | tf_op jit(solution)/shard_map/reduce_scatter | solution.py:157
  (87 shorter events, 9.7 us)
Async XLA Ops:
  7.2 150.2 %copy-start = (bf16[128,1792]{1,0:T(8,128)(2,1)S(1)}, bf16[128,1792]{1,0:T(8,128)(2,1)}, u32[]{:S(2)}) copy-start(bf16[128,1792]{1,0:T(8,128)(2,1)} %param.14) | copy-start | bytes 1376260
  7.2 213.4 %reduce-scatter.10.cloned.1.call-start = ((), (), s32[]{:S(2)}) async-start(), calls=%async_computation.4 | async-start | bytes 3342336 | tf_op jit(solution)/shard_map/reduce_scatter | solution.py:146
  7.2 97.3 %collective-permute-start = (bf16[1,150,3584]{2,1,0:T(8,128)(2,1)}, bf16[1,150,3584]{2,1,0:T(8,128)(2,1)}, u32[]{:S(2)}, u32[]{:S(2)}) collective-permute-start(bf16[1,150,3584]{2,1,0:T(8,128)(2,1)} %param.12), channel_id=1, source_target_pairs={{0,16},{16,32},{32,48},{48,64},{64,80},{80,96},{96,112},{112,128},... | collective-permute-start | bytes 3225608 | tf_op jit(solution)/shard_map/ppermute | solution.py:19
  54.8 7.5 %copy-start.9 = (bf16[1,192,224]{2,1,0:T(8,128)(2,1)S(1)}, bf16[1,192,224]{2,1,0:T(8,128)(2,1)}, u32[]{:S(2)}) copy-start(bf16[1,192,224]{2,1,0:T(8,128)(2,1)} %param.11) | copy-start | bytes 258052
  58.7 45.6 %copy-start.2 = (bf16[1,192,1792]{2,1,0:T(8,128)(2,1)}, bf16[1,192,1792]{2,1,0:T(8,128)(2,1)S(1)}, u32[]{:S(2)}) copy-start(bf16[1,192,1792]{2,1,0:T(8,128)(2,1)S(1)} %copy.24) | copy-start | bytes 2064388
  62.4 41.8 %copy-start.16 = (s32[1,3072]{1,0:T(1,128)S(1)}, s32[1,3072]{1,0:T(1,128)}, u32[]{:S(2)}) copy-start(s32[1,3072]{1,0:T(1,128)} %param.18) | copy-start | bytes 36868
  62.4 42.1 %copy-start.21 = (s32[1,192]{1,0:T(1,128)S(1)}, s32[1,192]{1,0:T(1,128)}, u32[]{:S(2)}) copy-start(s32[1,192]{1,0:T(1,128)} %param.17) | copy-start | bytes 2308
  104.5 2.6 copy-start.14
  104.6 2.6 copy-start.3
  107.2 1.6 copy-start.1
  108.6 30.9 %copy-start.5 = (bf16[192,1792,1]{1,0,2:T(8,128)(2,1)}, bf16[192,1792,1]{1,0,2:T(8,128)(2,1)S(1)}, u32[]{:S(2)}) copy-start(bf16[192,1792,1]{1,0,2:T(8,128)(2,1)S(1)} %get-tuple-element.8) | copy-start | bytes 2064388
  108.6 0.9 copy-start.20
  108.6 30.0 %copy-start.22 = (f32[1,128]{1,0:T(1,128)S(1)}, f32[1,128]{1,0:T(1,128)}, u32[]{:S(2)}) copy-start(f32[1,128]{1,0:T(1,128)} %param.15) | copy-start | bytes 1540
  109.5 29.1 %copy-start.18 = (f32[192]{0:T(256)}, f32[192]{0:T(256)S(1)}, u32[]{:S(2)}) copy-start(f32[192]{0:T(256)S(1)} %add_rsqrt_fusion) | copy-start | bytes 2308
  138.4 18.0 %copy-start.7 = (bf16[1,3072,1,128]{3,1,2,0:T(8,128)(2,1)}, bf16[1,3072,1,128]{3,1,2,0:T(8,128)(2,1)S(1)}, u32[]{:S(2)}) copy-start(bf16[1,3072,1,128]{3,1,2,0:T(8,128)(2,1)S(1)} %all_gather.18) | copy-start | bytes 2359300
  138.6 22.6 %copy-start.19 = (f32[192]{0:T(256)}, f32[192]{0:T(256)S(1)}, u32[]{:S(2)}) copy-start(f32[192]{0:T(256)S(1)} %add_rsqrt_fusion.1) | copy-start | bytes 2308
  139.5 17.9 %copy-start.4 = (bf16[1,192,1792]{2,1,0:T(8,128)(2,1)S(1)}, bf16[1,192,1792]{2,1,0:T(8,128)(2,1)}, u32[]{:S(2)}) copy-start(bf16[1,192,1792]{2,1,0:T(8,128)(2,1)} %copy.28) | copy-start | bytes 2064388
  157.8 1.2 copy-start.17
  160.0 5.2 copy-start.12
  161.2 1.1 copy-start.6
  165.2 139.4 %reduce-scatter.14.cloned.1.call-start = ((), (), s32[]{:S(2)}) async-start(), calls=%async_computation.7 | async-start | bytes 2064384
  171.7 3.1 copy-start.23
  174.6 267.3 %all-gather.4.cloned.1.call-start = ((), (), s32[]{:S(2)}) async-start(), calls=%async_computation.6 | async-start | bytes 12386304 | tf_op jit(solution)/shard_map/all_gather | solution.py:11
  222.9 3.1 copy-start.13
  225.9 335.0 %reduce-scatter.16.cloned.1.call-start = ((), (), s32[]{:S(2)}) async-start(), calls=%async_computation.8 | async-start | bytes 946176
  228.5 458.1 %reduce-scatter.12.cloned.1.call-start = ((), (), s32[]{:S(2)}) async-start(), calls=%async_computation.5 | async-start | bytes 2838528 | tf_op jit(solution)/shard_map/reduce_scatter | solution.py:157
  441.9 6.0 copy-start.15
  447.9 2.0 copy-start.10
  447.9 3.9 copy-start.8
  447.9 3.9 copy-start.11
Sparse Core Ops, SparseCore 0:
  165.3 55.2 reduce-scatter.9
  224.6 79.9 reduce-scatter.13
  307.2 134.6 all-gather.3
  444.8 116.0 reduce-scatter.15
  563.9 122.6 reduce-scatter.11
